TPU v7x, 32 devices: a whole 2x2x4 slice. The times are simulated.
32 devices in a mesh: dp: 8 (over z, y), seq: 4 (over x, core).
Axes of the slice: x: 2, y: 2, z: 4, core: 2. Of those that a mesh axis runs over, the one named last changes fastest.
Arguments:
- hidden_states: bfloat16 [4096, 2048], P(('dp', 'seq'))
- query_weight: bfloat16 [2048, 512], P('dp')
- key_weight: bfloat16 [2048, 128], P('dp')
- value_weight: bfloat16 [2048, 128], P('dp'), may hold values from -0.125 to 0.125
- doc_lengths: int32 [8, 8], P('dp'), may hold values from 1 to 256, 512 in all within a row
Outputs:
- context: bfloat16 [4096, 512], P(('dp', 'seq'))
Inputs may be any that keep to these rules, and one draw needn't show every extreme that they name: `doc_lengths`: each row sums to 512, and its longest document has exactly 256 tokens.
All inputs are finite; a program needn't handle non-finite values.
Results may differ from a plain program's by a relative error of at most 0.0076.
Values may be sent and summed in bfloat16 or wider, within the bound.
A program may use at most 64 MiB of HBM per device.

v0:
```python
import math
import jax
import jax.numpy as jnp
from jax import lax
from jax.sharding import PartitionSpec as P

HD = 64
EPSILON = 1e-05
THETA = 500000.0
NEG_FILL = -1e30


def normalize(states):
    floats = states.astype(jnp.float32)
    scale = lax.rsqrt(jnp.mean(floats * floats, axis=-1, keepdims=True) + EPSILON)
    return (floats * scale).astype(jnp.bfloat16)


def doc_offsets(doc_sizes, positions):
    ends = jnp.cumsum(doc_sizes)
    before = (ends[None, :] <= positions[:, None]).astype(jnp.int32)
    docs = jnp.sum(before, axis=1)
    starts = jnp.sum(before * doc_sizes[None, :], axis=1)
    return (docs, positions - starts)


def rotate(vectors, offset):
    half_dim = vectors.shape[-1] // 2
    index = jnp.arange(half_dim, dtype=jnp.float32)
    freqs = jnp.exp(index * (-2.0 / vectors.shape[-1]) * math.log(THETA))
    angle = offset.astype(jnp.float32)[:, None] * freqs[None, :]
    cosine = jnp.cos(angle)[:, None, :]
    sine = jnp.sin(angle)[:, None, :]
    first = vectors[..., :half_dim]
    second = vectors[..., half_dim:]
    return jnp.concatenate(
        [first * cosine - second * sine, second * cosine + first * sine], axis=-1
    )


def attend(queries, keys, values, docs):
    seq_length = queries.shape[0]
    group = queries.shape[1]
    scale = queries.shape[-1] ** (-0.5)
    block = math.gcd(256, seq_length)
    key_pos = jnp.arange(seq_length, dtype=jnp.int32)

    def one_block(number):
        first_row = number * block
        query_block = lax.dynamic_slice_in_dim(queries, first_row, block, 0)
        query_docs = lax.dynamic_slice_in_dim(docs, first_row, block, 0)
        query_pos = first_row + jnp.arange(block, dtype=jnp.int32)
        scores = (
            jnp.einsum("qgd,kd->gqk", query_block, keys, preferred_element_type=jnp.float32) * scale
        )
        allowed = (key_pos[None, :] <= query_pos[:, None]) & (docs[None, :] == query_docs[:, None])
        scores = jnp.where(allowed[None], scores, NEG_FILL)
        highest = jnp.max(scores, axis=-1, keepdims=True)
        expons = jnp.exp(scores - highest)
        totals = jnp.sum(expons, axis=-1, keepdims=True)
        weights = (expons / totals).astype(jnp.bfloat16)
        mixed = jnp.einsum("gqk,kd->qgd", weights, values, preferred_element_type=jnp.float32)
        return mixed.astype(jnp.bfloat16)

    blocks = lax.map(one_block, jnp.arange(seq_length // block, dtype=jnp.int32))
    return blocks.reshape(seq_length, group * queries.shape[-1])


def shards(hidden_states, query_weight, key_weight, value_weight, doc_lengths):
    tok_count = hidden_states.shape[0]
    seq_count = lax.axis_size("seq")
    seq_index = lax.axis_index("seq")
    seq_length = tok_count * seq_count
    head_dim = HD
    heads_here = query_weight.shape[1] // (head_dim * seq_count)
    kv_heads = key_weight.shape[1] // head_dim
    normed = normalize(hidden_states)
    doc_sizes = doc_lengths[0]
    all_positions = jnp.arange(seq_length, dtype=jnp.int32)
    docs_all, offset_all = doc_offsets(doc_sizes, all_positions)
    pieces = (
        lax.all_gather(query_weight, "dp", axis=0, tiled=True),
        lax.all_gather(key_weight, "dp", axis=0, tiled=True),
        lax.all_gather(value_weight, "dp", axis=0, tiled=True),
    )
    query_lin, key_lin, value_lin = tuple(
        (jnp.dot(normed, piece, preferred_element_type=jnp.float32) for piece in pieces)
    )
    own_offset = lax.dynamic_slice_in_dim(offset_all, seq_index * tok_count, tok_count, 0)
    query_rot = (
        rotate(query_lin.reshape(tok_count, -1, head_dim), own_offset)
        .astype(jnp.bfloat16)
        .reshape(tok_count, -1)
    )
    key_rot = rotate(key_lin.reshape(tok_count, kv_heads, head_dim), own_offset).astype(
        jnp.bfloat16
    )
    value_cast = value_lin.astype(jnp.bfloat16).reshape(tok_count, kv_heads, head_dim)
    key_value = jnp.concatenate([key_rot, value_cast], axis=2)
    repeated = jnp.repeat(key_value, seq_count // kv_heads, axis=1).reshape(tok_count, -1)
    query_heads, kv_local = (
        lax.all_to_all(query_rot, "seq", split_axis=1, concat_axis=0, tiled=True),
        lax.all_to_all(repeated, "seq", split_axis=1, concat_axis=0, tiled=True),
    )
    key_local = kv_local[:, :head_dim]
    value_local = kv_local[:, head_dim:]
    mixed_heads = attend(
        query_heads.reshape(seq_length, heads_here, head_dim), key_local, value_local, docs_all
    )
    return lax.all_to_all(mixed_heads, "seq", split_axis=0, concat_axis=1, tiled=True)


def solution(mesh):
    placed = (P(("dp", "seq"), None), P("dp", None), P("dp", None), P("dp", None), P("dp", None))
    return jax.shard_map(
        shards, mesh=mesh, in_specs=placed, out_specs=P(("dp", "seq"), None), check_vma=False
    )
```

profile of v0, /device:TPU:0, one launch (start us, length us, event | category | flops | bytes accessed | tf_op | source)
XLA Modules:
  0.0 120.7 jit_solution(3050384695510439155)
XLA Ops:
  6.5 0.0 copy-start
  6.5 0.0 copy-start.1
  6.5 0.0 all-gather.2.cloned.1.call-start
  6.5 0.7 all-gather.2.cloned.1.call-update
  7.3 0.8 reduce-window.8
  8.1 0.7 select_reduce_fusion
  8.9 0.1 dynamic-slice_convert_fusion
  8.9 1.2 %fusion.23 = f32[128]{0:T(128)S(1)} fusion(bf16[128,2048]{1,0:T(8,128)(2,1)} %param.7), kind=kLoop, calls=%fused_computation.27 | loop fusion | flops 786304 | bytes 524800 | tf_op jit(solution)/shard_map/reduce_sum | solution.py:15
  10.2 0.1 multiply_cosine_fusion
  10.3 34.1 %all_gather.10 = bf16[2048,128]{1,0:T(8,128)(2,1)S(1)} all-gather(bf16[256,128]{1,0:T(8,128)(2,1)} %param.9), channel_id=1, replica_groups=mesh['dp'=8,'seq'=4] {'dp'}, dimensions={0}, use_global_device_ids=true | all-gather | bytes 589824 | tf_op jit(solution)/shard_map/all_gather | solution.py:83
  44.5 1.4 %fusion.26 = f32[128,128]{0,1:T(8,128)S(1)} fusion(bf16[2048,128]{1,0:T(8,128)(2,1)S(1)} %all_gather.10, bf16[128,2048]{1,0:T(8,128)(2,1)} %param.7, f32[128]{0:T(128)S(1)} %add_rsqrt_fusion), kind=kOutput, calls=%fused_computation.44 | convolution fusion | flops 67895296 | bytes 1114624 | tf_op jit(solution)/shard_map/dot_general | solution.py:87
  45.9 0.0 copy-done.1
  45.9 32.3 %all_gather.11 = bf16[2048,128]{1,0:T(8,128)(2,1)S(1)} all-gather(bf16[256,128]{1,0:T(8,128)(2,1)S(1)} %copy-done.1), channel_id=1, replica_groups=mesh['dp'=8,'seq'=4] {'dp'}, dimensions={0}, use_global_device_ids=true | all-gather | bytes 589824 | tf_op jit(solution)/shard_map/all_gather | solution.py:84
  78.2 0.0 copy-done
  78.2 0.4 convolution_convert_fusion.1
  78.7 0.7 broadcast_in_dim.16
  79.3 3.3 %all-to-all-start.1 = ((bf16[128,4,128]{0,2,1:T(8,128)(2,1)}), bf16[128,4,128]{0,2,1:T(8,128)(2,1)S(1)}, u32[]{:S(2)}, u32[]{:S(2)}) async-start(bf16[128,4,128]{0,2,1:T(8,128)(2,1)} %bitcast.8), calls=%async_computation.1 | async-start | bytes 262144 | tf_op jit(solution)/shard_map/all_to_all | solution.py:103
  82.7 4.6 %all-to-all-done.1 = bf16[128,4,128]{0,2,1:T(8,128)(2,1)S(1)} async-done(((bf16[128,4,128]{0,2,1:T(8,128)(2,1)}), bf16[128,4,128]{0,2,1:T(8,128)(2,1)S(1)}, u32[]{:S(2)}, u32[]{:S(2)}) %all-to-all-start.1) | async-done | bytes 131104 | tf_op jit(solution)/shard_map/all_to_all | solution.py:103
  87.2 0.1 copy.34
  87.4 0.0 all-gather.2.cloned.1.call-done
  87.4 2.6 %fusion.28 = f32[128,512]{0,1:T(8,128)S(1)} fusion(bf16[2048,512]{1,0:T(8,128)(2,1)} %all-gather.2.cloned.1.call-done, bf16[128,2048]{1,0:T(8,128)(2,1)S(1)} %copy-done, f32[128]{0:T(128)S(1)} %add_rsqrt_fusion), kind=kOutput, calls=%fused_computation.45 | convolution fusion | flops 269221888 | bytes 2884096 | tf_op jit(solution)/shard_map/dot_general | solution.py:87
  90.0 0.7 pad_maximum_fusion
  90.7 3.3 %all-to-all-start = ((bf16[128,4,128]{0,2,1:T(8,128)(2,1)}), bf16[128,4,128]{0,2,1:T(8,128)(2,1)S(1)}, u32[]{:S(2)}, u32[]{:S(2)}) async-start(bf16[128,4,128]{0,2,1:T(8,128)(2,1)} %bitcast.4), calls=%async_computation | async-start | bytes 262144 | tf_op jit(solution)/shard_map/all_to_all | solution.py:102
  94.0 0.1 fusion.35
  94.1 0.1 copy.36
  94.2 0.1 copy.35
  94.3 4.2 %all-to-all-done = bf16[128,4,128]{0,2,1:T(8,128)(2,1)S(1)} async-done(((bf16[128,4,128]{0,2,1:T(8,128)(2,1)}), bf16[128,4,128]{0,2,1:T(8,128)(2,1)S(1)}, u32[]{:S(2)}, u32[]{:S(2)}) %all-to-all-start) | async-done | bytes 131104 | tf_op jit(solution)/shard_map/all_to_all | solution.py:102
  98.6 0.1 copy.33
  98.7 0.1 reshape.178
  98.7 7.1 %while.11 = (s32[]{:T(128)}, bf16[2,256,2,64]{1,3,2,0:T(8,128)(2,1)S(1)}, s32[2]{0:T(128)S(1)}, s32[512]{0:T(512)S(1)}, bf16[512,2,64]{0,2,1:T(8,128)(2,1)S(1)},...) while((s32[]{:T(128)}, ...), condition=%wide.region_7.8_spmd.clone, body=%wide.region_4.7_spmd.clone.sunk | while | flops 103450368 | bytes 3943619 | solution.py:65
  98.8 0.6 dynamic_slice.31
  100.0 0.1 dynamic_slice.32
  100.1 0.2 fusion.56
  100.3 0.6 fusion.57
  100.9 0.3 fusion.58
  101.2 1.1 fusion.59
  102.3 0.6 dynamic_slice.31
  103.6 0.1 dynamic_slice.32
  103.7 0.2 fusion.56
  103.8 0.6 fusion.57
  104.4 0.3 fusion.58
  104.8 1.1 fusion.59
  105.9 0.1 copy.37
  106.0 0.1 all_to_all.44
  106.1 7.0 %all_to_all.51 = bf16[4,128,128]{1,2,0:T(8,128)(2,1)S(1)} all-to-all(bf16[4,128,128]{1,2,0:T(8,128)(2,1)S(1)} %copy.38), channel_id=1, replica_groups=mesh['dp'=8,'seq'=4] {'seq'}, dimensions={0} | all-to-all | bytes 262144 | tf_op jit(solution)/shard_map/all_to_all | solution.py:110
  113.1 0.8 copy.39
  (11 shorter events, 0.1 us)
Async XLA Ops:
  6.5 71.7 %copy-start = (bf16[128,2048]{1,0:T(8,128)(2,1)S(1)}, bf16[128,2048]{1,0:T(8,128)(2,1)}, u32[]{:S(2)}) copy-start(bf16[128,2048]{1,0:T(8,128)(2,1)} %param.7) | copy-start | bytes 1572868
  6.5 39.4 %copy-start.1 = (bf16[256,128]{1,0:T(8,128)(2,1)S(1)}, bf16[256,128]{1,0:T(8,128)(2,1)}, u32[]{:S(2)}) copy-start(bf16[256,128]{1,0:T(8,128)(2,1)} %param.10) | copy-start | bytes 196612
  6.5 80.8 %all-gather.2.cloned.1.call-start = ((), (), s32[]{:S(2)}) async-start(), calls=%async_computation.3 | async-start | bytes 2359296 | tf_op jit(solution)/shard_map/all_gather | solution.py:82
  79.3 7.9 %all-to-all-start.1 = ((bf16[128,4,128]{0,2,1:T(8,128)(2,1)}), bf16[128,4,128]{0,2,1:T(8,128)(2,1)S(1)}, u32[]{:S(2)}, u32[]{:S(2)}) async-start(bf16[128,4,128]{0,2,1:T(8,128)(2,1)} %bitcast.8), calls=%async_computation.1 | async-start | bytes 262144 | tf_op jit(solution)/shard_map/all_to_all | solution.py:103
  90.7 7.9 %all-to-all-start = ((bf16[128,4,128]{0,2,1:T(8,128)(2,1)}), bf16[128,4,128]{0,2,1:T(8,128)(2,1)S(1)}, u32[]{:S(2)}, u32[]{:S(2)}) async-start(bf16[128,4,128]{0,2,1:T(8,128)(2,1)} %bitcast.4), calls=%async_computation | async-start | bytes 262144 | tf_op jit(solution)/shard_map/all_to_all | solution.py:102
Sparse Core Ops, SparseCore 0:
  9.5 57.2 all-gather.1
where the time goes:
time: 121 us
  blocking collectives  73.4 us (61%)
  between operations  13.6 us (11%)
  waiting for transfers between devices  9.54 us (8%)
  matrix products  8.37 us (7%)
  starting transfers between devices  6.65 us (5%)
  other arithmetic  4.16 us (3%)
  local copies, waits for them, and re-layouts  3.63 us (3%)
  loops' own time  1.41 us (1%)
    all_gather x1, blocking collectives, shards(): lax.all_gather(key_weight, 'dp', axis=0, tiled=True)  34.1 us
    all_gather x1, blocking collectives, shards(): lax.all_gather(value_weight, 'dp', axis=0, tiled=True)  32.3 us
    all_to_all x1, blocking collectives, shards(): lax.all_to_all(mixed_heads, 'seq', split_axis=0, concat_axis=1, tiled=True)  6.99 us
    all_to_all x1, waiting for transfers between devices, shards(): lax.all_to_all(repeated, 'seq', split_axis=1, concat_axis=0, tiled=True)  4.56 us
    dot_general x3, matrix products, shards(): jnp.dot(normed, piece, preferred_element_type=jnp.float32)  4.36 us
    all_to_all x1, waiting for transfers between devices, shards(): lax.all_to_all(query_rot, 'seq', split_axis=1, concat_axis=0, tiled=True)  4.25 us
    all_to_all x1, starting transfers between devices, shards(): lax.all_to_all(repeated, 'seq', split_axis=1, concat_axis=0, tiled=True)  3.33 us
    all_to_all x1, starting transfers between devices, shards(): lax.all_to_all(query_rot, 'seq', split_axis=1, concat_axis=0, tiled=True)  3.33 us
  transfers between devices with their start and end apart: 3, of which 2 were waited for; matrix products, arithmetic and copies ran while one was open for 5% of the time, Pallas kernels for 0%

commit v1 on v0

--- a/solution.py
+++ b/solution.py
@@ -8,6 +8,13 @@
 EPSILON = 1e-05
 THETA = 500000.0
 NEG_FILL = -1e30
+
+
+def lane_guide(vals):
+    state_now = jnp.concatenate(
+        lax.all_to_all(jnp.stack(jnp.split(vals, lax.psum(1, "seq"), axis=1)), "seq", 0, 0), axis=0
+    )
+    return state_now
 
 
 def normalize(states):
@@ -99,7 +106,7 @@
     key_value = jnp.concatenate([key_rot, value_cast], axis=2)
     repeated = jnp.repeat(key_value, seq_count // kv_heads, axis=1).reshape(tok_count, -1)
     query_heads, kv_local = (
-        lax.all_to_all(query_rot, "seq", split_axis=1, concat_axis=0, tiled=True),
+        lane_guide(query_rot),
         lax.all_to_all(repeated, "seq", split_axis=1, concat_axis=0, tiled=True),
     )
     key_local = kv_local[:, :head_dim]

time: 121 us -> 122 us (level)
  no operation moved by 1% of the time
where the time goes in v1:
time: 122 us; the launch traced here: 121 us
  blocking collectives  73.4 us (60%)
  between operations  13.6 us (11%)
  waiting for transfers between devices  9.53 us (8%)
  matrix products  8.37 us (7%)
  starting transfers between devices  6.65 us (5%)
  other arithmetic  4.19 us (3%)
  local copies, waits for them, and re-layouts  4.15 us (3%)
  loops' own time  1.41 us (1%)
    all_gather x1, blocking collectives, shards(): lax.all_gather(key_weight, 'dp', axis=0, tiled=True)  34.1 us
    all_gather x1, blocking collectives, shards(): lax.all_gather(value_weight, 'dp', axis=0, tiled=True)  32.3 us
    all_to_all x1, blocking collectives, shards(): lax.all_to_all(mixed_heads, 'seq', split_axis=0, concat_axis=1, tiled=True)  6.99 us
    all_to_all x1, waiting for transfers between devices, shards(): lax.all_to_all(repeated, 'seq', split_axis=1, concat_axis=0, tiled=True)  4.56 us
    dot_general x3, matrix products, shards(): jnp.dot(normed, piece, preferred_element_type=jnp.float32)  4.36 us
    all_to_all x1, waiting for transfers between devices, lane_guide(): lax.all_to_all(jnp.stack(jnp.split(vals, lax.psum(1, 'seq'), axis=1)), 's...  4.25 us
    all_to_all x1, starting transfers between devices, shards(): lax.all_to_all(repeated, 'seq', split_axis=1, concat_axis=0, tiled=True)  3.33 us
    all_to_all x1, starting transfers between devices, lane_guide(): lax.all_to_all(jnp.stack(jnp.split(vals, lax.psum(1, 'seq'), axis=1)), 's...  3.33 us
  transfers between devices with their start and end apart: 3, of which 2 were waited for; matrix products, arithmetic and copies ran while one was open for 5% of the time, Pallas kernels for 0%

profile of v1, /device:TPU:0, one launch (start us, length us, event | category | flops | bytes accessed | tf_op | source)
XLA Modules:
  0.0 121.3 jit_solution(9731737674602260007)
XLA Ops:
  6.5 0.0 all-gather.2.cloned.1.call-start
  6.5 0.7 all-gather.2.cloned.1.call-update
  7.3 0.8 reduce-window.8
  8.1 0.7 select_reduce_fusion
  8.9 0.1 dynamic-slice_convert_fusion
  8.9 1.2 %fusion.23 = f32[128]{0:T(128)S(1)} fusion(bf16[128,2048]{1,0:T(8,128)(2,1)} %param.7), kind=kLoop, calls=%fused_computation.27 | loop fusion | flops 786304 | bytes 524800 | tf_op jit(solution)/shard_map/reduce_sum | solution.py:22
  10.2 0.1 multiply_cosine_fusion
  10.3 34.1 %all_gather.10 = bf16[2048,128]{1,0:T(8,128)(2,1)S(1)} all-gather(bf16[256,128]{1,0:T(8,128)(2,1)} %param.9), channel_id=1, replica_groups=mesh['dp'=8,'seq'=4] {'dp'}, dimensions={0}, use_global_device_ids=true | all-gather | bytes 589824 | tf_op jit(solution)/shard_map/all_gather | solution.py:90
  44.5 1.4 %fusion.26 = f32[128,128]{0,1:T(8,128)S(1)} fusion(bf16[2048,128]{1,0:T(8,128)(2,1)S(1)} %all_gather.10, bf16[128,2048]{1,0:T(8,128)(2,1)} %param.7, f32[128]{0:T(128)S(1)} %add_rsqrt_fusion), kind=kOutput, calls=%fused_computation.45 | convolution fusion | flops 67895296 | bytes 1114624 | tf_op jit(solution)/shard_map/dot_general | solution.py:94
  45.9 0.0 copy-done.1
  45.9 32.3 %all_gather.11 = bf16[2048,128]{1,0:T(8,128)(2,1)S(1)} all-gather(bf16[256,128]{1,0:T(8,128)(2,1)S(1)} %copy-done.1), channel_id=1, replica_groups=mesh['dp'=8,'seq'=4] {'dp'}, dimensions={0}, use_global_device_ids=true | all-gather | bytes 589824 | tf_op jit(solution)/shard_map/all_gather | solution.py:91
  78.2 0.0 copy-done
  78.2 0.4 convolution_convert_fusion.1
  78.7 0.7 broadcast_in_dim.16
  79.3 3.3 %all-to-all-start.1 = ((bf16[128,4,128]{0,2,1:T(8,128)(2,1)}), bf16[128,4,128]{0,2,1:T(8,128)(2,1)S(1)}, u32[]{:S(2)}, u32[]{:S(2)}) async-start(bf16[128,4,128]{0,2,1:T(8,128)(2,1)} %bitcast.11), calls=%async_computation.1 | async-start | bytes 262144 | tf_op jit(solution)/shard_map/all_to_all | solution.py:110
  82.7 4.6 %all-to-all-done.1 = bf16[128,4,128]{0,2,1:T(8,128)(2,1)S(1)} async-done(((bf16[128,4,128]{0,2,1:T(8,128)(2,1)}), bf16[128,4,128]{0,2,1:T(8,128)(2,1)S(1)}, u32[]{:S(2)}, u32[]{:S(2)}) %all-to-all-start.1) | async-done | bytes 131104 | tf_op jit(solution)/shard_map/all_to_all | solution.py:110
  87.2 0.1 copy.58
  87.4 0.0 all-gather.2.cloned.1.call-done
  87.4 2.6 %fusion.28 = f32[128,512]{0,1:T(8,128)S(1)} fusion(bf16[2048,512]{1,0:T(8,128)(2,1)} %all-gather.2.cloned.1.call-done, bf16[128,2048]{1,0:T(8,128)(2,1)S(1)} %copy-done, f32[128]{0:T(128)S(1)} %add_rsqrt_fusion), kind=kOutput, calls=%fused_computation.46 | convolution fusion | flops 269221888 | bytes 2884096 | tf_op jit(solution)/shard_map/dot_general | solution.py:94
  90.0 0.1 copy.53
  90.2 0.1 copy.56
  90.3 0.1 copy.55
  90.4 0.1 copy.54
  90.5 0.7 pad_maximum_fusion.1
  91.2 3.3 %all-to-all-start = ((bf16[4,128,128]{2,1,0:T(8,128)(2,1)}), bf16[4,128,128]{2,1,0:T(8,128)(2,1)S(1)}, u32[]{:S(2)}, u32[]{:S(2)}) async-start(bf16[4,128,128]{2,1,0:T(8,128)(2,1)} %pad_maximum_fusion.1), calls=%async_computation | async-start | bytes 262144 | tf_op jit(solution)/shard_map/all_to_all | solution.py:15
  94.5 0.1 fusion.35
  94.7 0.1 copy.60
  94.8 0.1 copy.59
  94.9 4.2 %all-to-all-done = bf16[4,128,128]{2,1,0:T(8,128)(2,1)S(1)} async-done(((bf16[4,128,128]{2,1,0:T(8,128)(2,1)}), bf16[4,128,128]{2,1,0:T(8,128)(2,1)S(1)}, u32[]{:S(2)}, u32[]{:S(2)}) %all-to-all-start) | async-done | bytes 131104 | tf_op jit(solution)/shard_map/all_to_all | solution.py:15
  99.1 0.1 copy.57
  99.3 0.1 reshape_reshape.4
  99.3 7.1 %while.11 = (s32[]{:T(128)}, bf16[2,256,2,64]{1,3,2,0:T(8,128)(2,1)S(1)}, s32[2]{0:T(128)S(1)}, s32[512]{0:T(512)S(1)}, bf16[512,2,64]{0,2,1:T(8,128)(2,1)S(1)},...) while((s32[]{:T(128)}, ...), condition=%wide.region_7.8_spmd.clone, body=%wide.region_4.7_spmd.clone.sunk | while | flops 103450368 | bytes 3943619 | solution.py:72
  99.4 0.6 dynamic_slice.31
  100.6 0.1 dynamic_slice.32
  100.7 0.2 fusion.57
  100.9 0.6 fusion.58
  101.4 0.3 fusion.59
  101.8 1.1 fusion.60
  102.9 0.6 dynamic_slice.31
  104.2 0.1 dynamic_slice.32
  104.3 0.2 fusion.57
  104.4 0.6 fusion.58
  105.0 0.3 fusion.59
  105.4 1.1 fusion.60
  106.5 0.1 copy.61
  106.6 0.1 all_to_all.36
  106.7 7.0 %all_to_all.43 = bf16[4,128,128]{1,2,0:T(8,128)(2,1)S(1)} all-to-all(bf16[4,128,128]{1,2,0:T(8,128)(2,1)S(1)} %copy.62), channel_id=1, replica_groups=mesh['dp'=8,'seq'=4] {'seq'}, dimensions={0} | all-to-all | bytes 262144 | tf_op jit(solution)/shard_map/all_to_all | solution.py:117
  113.7 0.8 copy.63
  (15 shorter events, 0.1 us)
Async XLA Ops:
  6.5 71.7 %copy-start = (bf16[128,2048]{1,0:T(8,128)(2,1)S(1)}, bf16[128,2048]{1,0:T(8,128)(2,1)}, u32[]{:S(2)}) copy-start(bf16[128,2048]{1,0:T(8,128)(2,1)} %param.7) | copy-start | bytes 1572868
  6.5 39.4 %copy-start.1 = (bf16[256,128]{1,0:T(8,128)(2,1)S(1)}, bf16[256,128]{1,0:T(8,128)(2,1)}, u32[]{:S(2)}) copy-start(bf16[256,128]{1,0:T(8,128)(2,1)} %param.10) | copy-start | bytes 196612
  6.5 80.8 %all-gather.2.cloned.1.call-start = ((), (), s32[]{:S(2)}) async-start(), calls=%async_computation.3 | async-start | bytes 2359296 | tf_op jit(solution)/shard_map/all_gather | solution.py:89
  79.3 7.9 %all-to-all-start.1 = ((bf16[128,4,128]{0,2,1:T(8,128)(2,1)}), bf16[128,4,128]{0,2,1:T(8,128)(2,1)S(1)}, u32[]{:S(2)}, u32[]{:S(2)}) async-start(bf16[128,4,128]{0,2,1:T(8,128)(2,1)} %bitcast.11), calls=%async_computation.1 | async-start | bytes 262144 | tf_op jit(solution)/shard_map/all_to_all | solution.py:110
  91.2 7.9 %all-to-all-start = ((bf16[4,128,128]{2,1,0:T(8,128)(2,1)}), bf16[4,128,128]{2,1,0:T(8,128)(2,1)S(1)}, u32[]{:S(2)}, u32[]{:S(2)}) async-start(bf16[4,128,128]{2,1,0:T(8,128)(2,1)} %pad_maximum_fusion.1), calls=%async_computation | async-start | bytes 262144 | tf_op jit(solution)/shard_map/all_to_all | solution.py:15
Sparse Core Ops, SparseCore 0:
  9.5 57.2 all-gather.1
